TPU v7x, 512 devices: a whole 4x8x8 slice. The times are simulated.
512 devices in a mesh: src: 4 (over z_lo), shard: 16 (over y, core), slab: 8 (over z_hi, x).
Axes of the slice: x: 4, y: 8, z: 8 (z_hi: 2, z_lo: 4; z = z_hi * 4 + z_lo), core: 2. Of those that a mesh axis runs over, the one named last changes fastest.
Arguments:
- src_feat: bfloat16 [4, 256, 256, 256], P('src', 'slab', 'shard'), may hold values from -6 to 6
- coords: int32 [4, 2], P('src'), may hold values from 0 to 6
- offsets: int32 [8], P('slab'), may hold values from 0 to 2128
- weights: bfloat16 [4, 2, 9, 512, 128], P('src'), may hold values from -0.09375 to 0.09375
Outputs:
- target_feat: bfloat16 [4, 256, 256, 256], P('src', 'slab', 'shard')
All inputs are finite; a program needn't handle non-finite values.
Results may differ from a plain program's by a relative error of at most 0.0047.
Values may be sent and summed in bfloat16 or wider, within the bound.
A program may use at most 64 MiB of HBM per device.

v0:
```python
import math

import jax
import jax.numpy as jnp
from jax import lax
from jax.sharding import PartitionSpec as P


def with_halo(shard, sides, width):
    for axis, dim in sides:
        size, length = (lax.axis_size(axis), shard.shape[dim])
        up = [(i, (i + 1) % size) for i in range(size - 1)]
        down = [(j, i) for i, j in up]
        last = lax.slice_in_dim(shard, length - width, length, axis=dim)
        leading = lax.slice_in_dim(shard, 0, width, axis=dim)
        before = lax.ppermute(last, axis, up)
        after = lax.ppermute(leading, axis, down)
        shard = jnp.concatenate([before, shard, after], axis=dim)
    return shard


def encoding(rowpos, chan_count):
    channel_idx = jnp.arange(chan_count, dtype=jnp.int32)
    halves = (channel_idx // 2).astype(jnp.float32)
    frequency = jnp.exp(-math.log(1000.0) * halves / (chan_count / 2))
    phases = (channel_idx % 2).astype(jnp.float32) * (math.pi / 2)
    return jnp.sin(rowpos.astype(jnp.float32)[:, None] * frequency[None, :] + phases[None, :])


def blend_weights(coords):
    vertical = coords[:, 0].astype(jnp.float32) / 6.0
    across = coords[:, 1].astype(jnp.float32) / 6.0
    return jnp.stack(
        [
            (1.0 - vertical) * (1.0 - across),
            (1.0 - vertical) * across,
            vertical * (1.0 - across),
            vertical * across,
        ],
        axis=1,
    )


def local(src_feat, coords, offsets, weights):
    row_count = src_feat.shape[1]
    col_count = src_feat.shape[2]
    chan_count = src_feat.shape[3]
    rowpos = offsets[0] + jnp.arange(row_count, dtype=jnp.int32)
    encoded = encoding(rowpos, chan_count)
    posed = (src_feat.astype(jnp.float32) + encoded[None, :, None, :]).astype(jnp.bfloat16)
    all_views = lax.all_gather(posed, "src", axis=0, tiled=True)
    padded = with_halo(all_views, (("shard", 2), ("slab", 1)), 1)
    view_count = padded.shape[0]
    targets = weights.shape[0]
    groups = weights.shape[1]
    out_width = weights.shape[4]
    per_group = view_count // groups
    grouped = padded.reshape(groups, per_group, row_count + 2, col_count + 2, chan_count)
    grouped = grouped.transpose(0, 2, 3, 1, 4).reshape(
        groups, row_count + 2, col_count + 2, per_group * chan_count
    )
    convolved = jnp.zeros((targets, groups, row_count, col_count, out_width), jnp.float32)
    for tap_index in range(9):
        tap_row = tap_index // 3
        tap_col = tap_index % 3
        window = grouped[:, tap_row : tap_row + row_count, tap_col : tap_col + col_count, :]
        convolved = convolved + jnp.einsum(
            "grcn,tgno->tgrco", window, weights[:, :, tap_index], preferred_element_type=jnp.float32
        )
    convolved = convolved.transpose(0, 2, 3, 1, 4).reshape(
        targets, row_count, col_count, groups * out_width
    )
    mixing = blend_weights(coords)
    own_views = padded[:, 1:-1, 1:-1, :]
    blended = jnp.zeros((targets, row_count, col_count, chan_count), jnp.float32)
    for view_index in range(view_count):
        blended = (
            blended
            + mixing[:, view_index, None, None, None]
            * own_views[view_index].astype(jnp.float32)[None]
        )
    return (blended + jax.nn.silu(convolved)).astype(jnp.bfloat16)


def solution(mesh):
    in_specs = (
        P("src", "slab", "shard", None),
        P("src", None),
        P("slab"),
        P("src", None, None, None, None),
    )
    out_specs = P("src", "slab", "shard", None)
    return jax.shard_map(local, mesh=mesh, in_specs=in_specs, out_specs=out_specs, check_vma=False)
```

profile of v0, /device:TPU:31, one launch (start us, length us, event | category | flops | bytes accessed | tf_op | source)
XLA Modules:
  0.0 106.5 jit_solution(3161733872161110373)
XLA Ops:
  7.4 1.7 %add_convert_fusion.1 = bf16[1,32,16,256]{3,2,1,0:T(8,128)(2,1)} fusion(bf16[1,32,16,256]{3,2,1,0:T(8,128)(2,1)} %param.4, f32[32,256]{1,0:T(8,128)S(1)} %add_sine_fusion), kind=kLoop, calls=%fused_computation.22 | loop fusion | flops 393216 | bytes 557056 | tf_op jit(solution)/shard_map/convert_element_type | solution.py:50
  9.1 41.0 %all-gather.2.cloned.1.call-done = bf16[4,32,16,256]{3,2,1,0:T(8,128)(2,1)} async-done(((bf16[1,32,16,256]{3,2,1,0:T(8,128)(2,1)}), bf16[4,32,16,256]{3,2,1,0:T(8,128)(2,1)}) %all-gather.2.cloned.1.call-update) | async-done | bytes 1048592 | tf_op jit(solution)/shard_map/all_gather | solution.py:51
  50.2 1.5 %fusion.37 = (bf16[4,32,1,256]{3,2,1,0:T(2,128)(2,1)S(1)}, bf16[4,32,1,256]{3,2,1,0:T(2,128)(2,1)S(1)}) fusion(bf16[4,32,16,256]{3,2,1,0:T(8,128)(2,1)} %all-gather.2.cloned.1.call-done), kind=kLoop, calls=%fused_computation.59 | loop fusion | bytes 262144 | tf_op jit(solution)/shard_map/slice | solution.py:14
  51.7 5.1 %collective-permute-start = (bf16[4,32,1,256]{3,2,1,0:T(2,128)(2,1)S(1)}, bf16[4,32,1,256]{3,2,1,0:T(2,128)(2,1)S(1)}, u32[]{:S(2)}, u32[]{:S(2)}) collective-permute-start(bf16[4,32,1,256]{3,2,1,0:T(2,128)(2,1)S(1)} %get-tuple-element.16), channel_id=1, source_target_pairs={{0,8},{8,16},{16,24},{24,32},{32,40},{40,48},{48,56},{56,64},{64,7... | collective-permute-start | bytes 196616 | tf_op jit(solution)/shard_map/ppermute | solution.py:16
  56.8 1.9 %collective-permute-start.1 = (bf16[4,32,1,256]{3,2,1,0:T(2,128)(2,1)S(1)}, bf16[4,32,1,256]{3,2,1,0:T(2,128)(2,1)S(1)}, u32[]{:S(2)}, u32[]{:S(2)}) collective-permute-start(bf16[4,32,1,256]{3,2,1,0:T(2,128)(2,1)S(1)} %get-tuple-element.17), channel_id=1, source_target_pairs={{8,0},{16,8},{24,16},{32,24},{40,32},{48,40},{56,48},{64,56},{72,6... | collective-permute-start | bytes 196616 | tf_op jit(solution)/shard_map/ppermute | solution.py:17
  58.7 5.6 %collective-permute-done.1 = bf16[4,32,1,256]{3,2,1,0:T(2,128)(2,1)S(1)} collective-permute-done((bf16[4,32,1,256]{3,2,1,0:T(2,128)(2,1)S(1)}, bf16[4,32,1,256]{3,2,1,0:T(2,128)(2,1)S(1)}, u32[]{:S(2)}, u32[]{:S(2)}) %collective-permute-start.1) | collective-permute-done | bytes 65568 | tf_op jit(solution)/shard_map/ppermute | solution.py:17
  64.3 0.8 pad_maximum_fusion.3
  65.1 5.3 %collective-permute-start.2 = (bf16[4,1,18,256]{3,2,1,0:T(8,128)(2,1)S(1)}, bf16[4,1,18,256]{3,2,1,0:T(8,128)(2,1)S(1)}, u32[]{:S(2)}, u32[]{:S(2)}) collective-permute-start(bf16[4,1,18,256]{3,2,1,0:T(8,128)(2,1)S(1)} %get-tuple-element.5), channel_id=1, source_target_pairs={{0,1},{1,2},{2,3},{3,4},{4,5},{5,6},{6,7},{8,9},{9,10},{10,11},{11... | collective-permute-start | bytes 110600 | tf_op jit(solution)/shard_map/ppermute | solution.py:16
  70.4 1.9 %collective-permute-start.3 = (bf16[4,1,18,256]{3,2,1,0:T(8,128)(2,1)S(1)}, bf16[4,1,18,256]{3,2,1,0:T(8,128)(2,1)S(1)}, u32[]{:S(2)}, u32[]{:S(2)}) collective-permute-start(bf16[4,1,18,256]{3,2,1,0:T(8,128)(2,1)S(1)} %get-tuple-element.6), channel_id=1, source_target_pairs={{1,0},{2,1},{3,2},{4,3},{5,4},{6,5},{7,6},{9,8},{10,9},{11,10},{12... | collective-permute-start | bytes 110600 | tf_op jit(solution)/shard_map/ppermute | solution.py:17
  72.3 0.6 fusion.38
  74.3 7.0 %collective-permute-done.3 = bf16[4,1,18,256]{3,2,1,0:T(8,128)(2,1)S(1)} collective-permute-done((bf16[4,1,18,256]{3,2,1,0:T(8,128)(2,1)S(1)}, bf16[4,1,18,256]{3,2,1,0:T(8,128)(2,1)S(1)}, u32[]{:S(2)}, u32[]{:S(2)}) %collective-permute-start.3) | collective-permute-done | bytes 36896 | tf_op jit(solution)/shard_map/ppermute | solution.py:17
  81.2 1.1 %pad_maximum_fusion = bf16[4,34,18,256]{3,2,1,0:T(8,128)(2,1)S(1)} fusion(bf16[4,1,18,256]{3,2,1,0:T(8,128)(2,1)S(1)} %collective-permute-done.3, bf16[4,32,1,256]{3,2,1,0:T(2,128)(2,1)S(1)} %collective-permute-done.1, bf16[4,32,16,256]{3,2,1,0:T(8,128)(2,1)S(1)} %copy-done, bf16[4,32,1,256]{3,2,1,0:T(2,128)(2,1)S(1)} %collective-permute-done, ...), kind=kLoop, calls=%fused_computation | loop fusion | flops 6266880 | bytes 2506752 | tf_op jit(solution)/shard_map/concatenate | solution.py:18
  82.3 1.0 copy.130
  83.3 0.8 reshape.201
  84.2 10.1 %fusion.36 = (bf16[2,32,16,512]{3,0,2,1:T(2,128)(2,1)S(1)}, bf16[2,32,16,512]{3,0,2,1:T(2,128)(2,1)S(1)}, bf16[2,32,16,512]{3,0,2,1:T(2,128)(2,1)S(1)}, bf16[2,3...) fusion(bf16[2,34,18,512]{3,0,2,1:T(2,128)(2,1)S(1)} %reshape.201), kind=kLoop, calls=%fused_computation.58 | loop fusion | bytes 18874368 | tf_op jit(solution)/shard_map/slice | solution.py:66
  94.7 0.4 convolution_add_fusion.7
  95.1 0.4 convolution_add_fusion.6
  95.6 0.4 convolution_add_fusion.5
  96.0 0.4 convolution_add_fusion.4
  96.5 0.4 convolution_add_fusion.3
  96.9 0.4 convolution_add_fusion.2
  97.4 0.4 convolution_add_fusion.1
  97.8 0.4 fusion
  98.7 1.0 add_convert_fusion
  (15 shorter events, 1.1 us)
Async XLA Ops:
  6.5 65.8 %copy-start.2 = (s32[1,2]{1,0:T(1,128)S(1)}, s32[1,2]{1,0:T(1,128)}, u32[]{:S(2)}) copy-start(s32[1,2]{1,0:T(1,128)} %param.5) | copy-start | bytes 28
  6.5 43.6 %all-gather.2.cloned.1.call-start = ((), (), s32[]{:S(2)}) async-start(), calls=%async_computation | async-start | bytes 1310720 | tf_op jit(solution)/shard_map/all_gather | solution.py:51
  50.2 31.0 %copy-start = (bf16[4,32,16,256]{3,2,1,0:T(8,128)(2,1)S(1)}, bf16[4,32,16,256]{3,2,1,0:T(8,128)(2,1)}, u32[]{:S(2)}) copy-start(bf16[4,32,16,256]{3,2,1,0:T(8,128)(2,1)} %all-gather.2.cloned.1.call-done) | copy-start | bytes 3145732
  51.7 7.0 %collective-permute-start = (bf16[4,32,1,256]{3,2,1,0:T(2,128)(2,1)S(1)}, bf16[4,32,1,256]{3,2,1,0:T(2,128)(2,1)S(1)}, u32[]{:S(2)}, u32[]{:S(2)}) collective-permute-start(bf16[4,32,1,256]{3,2,1,0:T(2,128)(2,1)S(1)} %get-tuple-element.16), channel_id=1, source_target_pairs={{0,8},{8,16},{16,24},{24,32},{32,40},{40,48},{48,56},{56,64},{64,7... | collective-permute-start | bytes 196616 | tf_op jit(solution)/shard_map/ppermute | solution.py:16
  56.8 7.5 %collective-permute-start.1 = (bf16[4,32,1,256]{3,2,1,0:T(2,128)(2,1)S(1)}, bf16[4,32,1,256]{3,2,1,0:T(2,128)(2,1)S(1)}, u32[]{:S(2)}, u32[]{:S(2)}) collective-permute-start(bf16[4,32,1,256]{3,2,1,0:T(2,128)(2,1)S(1)} %get-tuple-element.17), channel_id=1, source_target_pairs={{8,0},{16,8},{24,16},{32,24},{40,32},{48,40},{56,48},{64,56},{72,6... | collective-permute-start | bytes 196616 | tf_op jit(solution)/shard_map/ppermute | solution.py:17
  65.1 9.1 %collective-permute-start.2 = (bf16[4,1,18,256]{3,2,1,0:T(8,128)(2,1)S(1)}, bf16[4,1,18,256]{3,2,1,0:T(8,128)(2,1)S(1)}, u32[]{:S(2)}, u32[]{:S(2)}) collective-permute-start(bf16[4,1,18,256]{3,2,1,0:T(8,128)(2,1)S(1)} %get-tuple-element.5), channel_id=1, source_target_pairs={{0,1},{1,2},{2,3},{3,4},{4,5},{5,6},{6,7},{8,9},{9,10},{10,11},{11... | collective-permute-start | bytes 110600 | tf_op jit(solution)/shard_map/ppermute | solution.py:16
  70.4 10.9 %collective-permute-start.3 = (bf16[4,1,18,256]{3,2,1,0:T(8,128)(2,1)S(1)}, bf16[4,1,18,256]{3,2,1,0:T(8,128)(2,1)S(1)}, u32[]{:S(2)}, u32[]{:S(2)}) collective-permute-start(bf16[4,1,18,256]{3,2,1,0:T(8,128)(2,1)S(1)} %get-tuple-element.6), channel_id=1, source_target_pairs={{1,0},{2,1},{3,2},{4,3},{5,4},{6,5},{7,6},{9,8},{10,9},{11,10},{12... | collective-permute-start | bytes 110600 | tf_op jit(solution)/shard_map/ppermute | solution.py:17
  84.2 10.1 %copy-start.1 = (bf16[1,2,9,512,128]{4,3,2,1,0:T(8,128)(2,1)S(1)}, bf16[1,2,9,512,128]{4,3,2,1,0:T(8,128)(2,1)}, u32[]{:S(2)}) copy-start(bf16[1,2,9,512,128]{4,3,2,1,0:T(8,128)(2,1)} %param.7) | copy-start | bytes 7077892
Sparse Core Ops, SparseCore 0:
  9.5 40.6 all-gather.1
where the time goes:
time: 107 us
  waiting for transfers between devices  53.6 us (50%)
  between operations  15.6 us (15%)
  local copies, waits for them, and re-layouts  14.4 us (13%)
  starting transfers between devices  14.2 us (13%)
  other arithmetic  4.85 us (5%)
  matrix products  3.96 us (4%)
    all_gather x1, waiting for transfers between devices, local(): all_views = lax.all_gather(posed, 'src', axis=0, tiled=True)  41 us
    ppermute x2, waiting for transfers between devices, with_halo(): after = lax.ppermute(leading, axis, down)  12.5 us
    ppermute x2, starting transfers between devices, with_halo(): before = lax.ppermute(last, axis, up)  10.4 us
    slice x1, local copies, waits for them, and re-layouts, local(): grouped[:, tap_row:tap_row + row_count, tap_col:tap_col + col_count, :]  10.1 us
    dot_general x9, matrix products, local(): jnp.einsum('grcn,tgno->tgrco', window, weights[:, :, tap_index], preferre...  3.96 us
    ppermute x2, starting transfers between devices, with_halo(): after = lax.ppermute(leading, axis, down)  3.84 us
  transfers between devices with their start and end apart: 5, of which 3 were waited for; matrix products, arithmetic and copies ran while one was open for 1% of the time, Pallas kernels for 0%

commit v1 on v0

v1 whole, which is shorter than its diff:
```python
import functools
import math

import jax
import jax.numpy as jnp
from jax import lax
from jax.experimental import pallas as pl
from jax.experimental.pallas import tpu as pltpu
from jax.sharding import PartitionSpec as P

VIEWS = 4
CHUNKS = 4
EDGE = 8
MESH = pl.DeviceIdType.MESH


def encoding(offset, first_row, row_count, chans):
    row_idx = lax.broadcasted_iota(jnp.int32, (row_count, chans), 0)
    rowpos = (offset + first_row + row_idx).astype(jnp.float32)
    chan = lax.broadcasted_iota(jnp.int32, (row_count, chans), 1)
    halves = (chan // 2).astype(jnp.float32)
    frequency = jnp.exp(-math.log(1000.0) * halves / (chans / 2))
    phases = (chan % 2).astype(jnp.float32) * (math.pi / 2)
    return jnp.sin(rowpos * frequency + phases)


def kernel(sizes, coords_ref, offsets_ref, src_hbm, w_ref, out_ref, src_ref, panel, weights, acc_side, acc_mid,
           src_sem, w_sem, z_send, z_recv, col_send, col_recv, row_send, row_recv):
    shards, slabs = sizes
    rows, cols, chans = src_ref.shape
    groups, _, depth, width = w_ref.shape
    chunk_rows = rows // CHUNKS
    s, h, b = lax.axis_index("src"), lax.axis_index("shard"), lax.axis_index("slab")
    below, above = s > 0, s < VIEWS - 1
    has_left, has_right = h > 0, h < shards - 1
    has_top, has_bottom = b > 0, b < slabs - 1
    partners = (
        (below, {"src": s - 1}), (above, {"src": s + 1}),
        (has_left, {"shard": h - 1}), (has_right, {"shard": h + 1}),
        (has_top, {"slab": b - 1}), (has_bottom, {"slab": b + 1}),
    )

    src_copy = pltpu.make_async_copy(src_hbm, src_ref, src_sem)
    src_copy.start()
    barrier = pltpu.get_barrier_semaphore()
    for present, target in partners:
        @pl.when(present)
        def _():
            pl.semaphore_signal(barrier, inc=1, device_id=target, device_id_type=MESH)

    def weight_copy(i):
        g, tap = i // 9, i % 9
        a, c = tap // 3, tap % 3
        lane = (0, 2, 1)[c] * width
        return pltpu.make_async_copy(
            w_ref.at[g, tap], weights.at[g, a, :, lane:lane + width], w_sem.at[i])

    for i in range(groups * 9):
        weight_copy(i).start()

    acc_side[...] = jnp.zeros_like(acc_side)
    acc_mid[...] = jnp.zeros_like(acc_mid)

    @pl.when(jnp.logical_not(has_left))
    def _():
        panel[:, 1:rows + 1, cols:cols + EDGE, :] = jnp.zeros((VIEWS, rows, EDGE, chans), panel.dtype)

    @pl.when(jnp.logical_not(has_right))
    def _():
        panel[:, 1:rows + 1, cols + EDGE:, :] = jnp.zeros((VIEWS, rows, EDGE, chans), panel.dtype)

    @pl.when(jnp.logical_not(has_top))
    def _():
        panel[:, 0] = jnp.zeros((VIEWS, cols + 2 * EDGE, chans), panel.dtype)

    @pl.when(jnp.logical_not(has_bottom))
    def _():
        panel[:, rows + 1] = jnp.zeros((VIEWS, cols + 2 * EDGE, chans), panel.dtype)

    src_copy.wait()
    pl.semaphore_wait(barrier, sum(present.astype(jnp.int32) for present, _ in partners))

    def chunk_start(k):
        return ((CHUNKS - 1) * k) % CHUNKS * chunk_rows

    def z_copy(v, k, up):
        part = panel.at[v, pl.ds(1 + chunk_start(k), chunk_rows), 0:cols, :]
        return pltpu.make_async_remote_copy(
            src_ref=part, dst_ref=part, send_sem=z_send.at[up, v, k], recv_sem=z_recv.at[v, k],
            device_id={"src": s + 1 if up else s - 1}, device_id_type=MESH)

    def col_copy(v, k, right):
        at = pl.ds(1 + chunk_start(k), chunk_rows)
        src = panel.at[v, at, cols - EDGE:cols, :] if right else panel.at[v, at, 0:EDGE, :]
        dst = panel.at[v, at, cols:cols + EDGE, :] if right else panel.at[v, at, cols + EDGE:, :]
        return pltpu.make_async_remote_copy(
            src_ref=src, dst_ref=dst, send_sem=col_send.at[right, v, k], recv_sem=col_recv.at[right, v, k],
            device_id={"shard": h + 1 if right else h - 1}, device_id_type=MESH)

    def row_copy(v, down):
        return pltpu.make_async_remote_copy(
            src_ref=panel.at[v, rows if down else 1], dst_ref=panel.at[v, 0 if down else rows + 1],
            send_sem=row_send.at[down, v], recv_sem=row_recv.at[down, v],
            device_id={"slab": b + 1 if down else b - 1}, device_id_type=MESH)

    def arrive(v, k, up, own):
        if own:
            start = chunk_start(k)
            encoded = encoding(offsets_ref[0], start, chunk_rows, chans)
            feat = src_ref[pl.ds(start, chunk_rows)].astype(jnp.float32)
            panel[v, pl.ds(1 + start, chunk_rows), 0:cols, :] = (feat + encoded[:, None, :]).astype(panel.dtype)
        else:
            z_copy(v, k, up).wait_recv()
        for direction, present in ((1, above), (0, below)):
            if own or direction == up:
                @pl.when(present)
                def _():
                    z_copy(v, k, direction).start()
        for right, present in ((1, has_right), (0, has_left)):
            @pl.when(present)
            def _():
                col_copy(v, k, right).start()

    def border(v, k):
        for right, present in ((1, has_left), (0, has_right)):
            @pl.when(present)
            def _():
                col_copy(v, k, right).wait_recv()

        @pl.when((k == 0) & has_top)
        def _():
            row_copy(v, 0).start()

        @pl.when((k == 1) & has_bottom)
        def _():
            row_copy(v, 1).start()

    def multiply(v, k):
        @pl.when(k == 0)
        def _():
            for down, present in ((1, has_top), (0, has_bottom)):
                @pl.when(present)
                def _():
                    row_copy(v, down).wait_recv()

        @pl.when(k < 3)
        def _():
            g = v // 2
            taken = pl.ds(pl.multiple_of((v % 2) * chans, chans), chans)
            full = panel[v, pl.ds(k, rows), :, :].reshape(rows * (cols + 2 * EDGE), chans)
            acc_side[g] += jnp.dot(full, weights[g, k, taken, 0:2 * width], preferred_element_type=jnp.float32)
            own = panel[v, pl.ds(k, rows), 0:cols, :].reshape(rows * cols, chans)
            acc_mid[g] += jnp.dot(own, weights[g, k, taken, 2 * width:], preferred_element_type=jnp.float32)

    def for_views(item, act, live):
        d, k = item // CHUNKS, item % CHUNKS

        @pl.when(live & (d == 0))
        def _():
            act(s, k, 1, True)

        @pl.when(live & (d > 0) & (s - d >= 0))
        def _():
            act(s - d, k, 1, False)

        @pl.when(live & (d > 0) & (s + d < VIEWS))
        def _():
            act(s + d, k, 0, False)

    items = VIEWS * CHUNKS
    lag = CHUNKS + 1

    @pl.loop(0, items + lag)
    def _(i):
        @pl.when(i == lag)
        def _():
            for n in range(groups * 9):
                weight_copy(n).wait()

        for_views(i, arrive, i < items)
        for_views(i - 1, lambda v, k, up, own: border(v, k), (i >= 1) & (i - 1 < items))
        for_views(i - lag, lambda v, k, up, own: multiply(v, k), i >= lag)

    vertical = coords_ref[0, 0].astype(jnp.float32) / 6.0
    across = coords_ref[0, 1].astype(jnp.float32) / 6.0
    mixing = ((1.0 - vertical) * (1.0 - across), (1.0 - vertical) * across,
              vertical * (1.0 - across), vertical * across)

    @pl.loop(0, rows // EDGE)
    def _(i):
        at = pl.ds(i * EDGE, EDGE)
        for g in range(groups):
            lanes = slice(g * width, (g + 1) * width)
            side = acc_side[g, pl.ds(pl.multiple_of(i * EDGE * (cols + 2 * EDGE), EDGE), EDGE * (cols + 2 * EDGE)), :]
            side = side.reshape(EDGE, cols + 2 * EDGE, 2 * width)
            joined = acc_mid[g, pl.ds(pl.multiple_of(i * EDGE * cols, EDGE), EDGE * cols), :].reshape(EDGE, cols, width)
            joined += jnp.concatenate([side[:, cols + EDGE - 1:cols + EDGE, :width], side[:, 0:cols - 1, :width]], axis=1)
            joined += jnp.concatenate([side[:, 1:cols, width:], side[:, cols + EDGE:cols + EDGE + 1, width:]], axis=1)
            blended = jnp.zeros((EDGE, cols, width), jnp.float32)
            for v in range(VIEWS):
                blended += mixing[v] * panel[v, pl.ds(1 + i * EDGE, EDGE), 0:cols, lanes].astype(jnp.float32)
            out_ref[at, :, lanes] = (blended + joined / (1.0 + jnp.exp(-joined))).astype(out_ref.dtype)

    for k in range(CHUNKS):
        for v in range(VIEWS):
            @pl.when(above & (s >= v))
            def _():
                z_copy(v, k, 1).wait_send()

            @pl.when(below & (s <= v))
            def _():
                z_copy(v, k, 0).wait_send()

            for right, present in ((1, has_right), (0, has_left)):
                @pl.when(present)
                def _():
                    col_copy(v, k, right).wait_send()
    for v in range(VIEWS):
        for down, present in ((1, has_bottom), (0, has_top)):
            @pl.when(present)
            def _():
                row_copy(v, down).wait_send()


def local(sizes, src_feat, coords, offsets, weights):
    _, rows, cols, chans = src_feat.shape
    _, groups, taps, depth, width = weights.shape
    wide = cols + 2 * EDGE
    dma = pltpu.SemaphoreType.DMA
    out = pl.pallas_call(
        functools.partial(kernel, sizes),
        out_shape=jax.ShapeDtypeStruct((rows, cols, chans), jnp.bfloat16),
        in_specs=[
            pl.BlockSpec(memory_space=pltpu.SMEM),
            pl.BlockSpec(memory_space=pltpu.SMEM),
            pl.BlockSpec(memory_space=pltpu.HBM),
            pl.BlockSpec(memory_space=pltpu.HBM),
        ],
        out_specs=pl.BlockSpec(memory_space=pltpu.VMEM),
        scratch_shapes=[
            pltpu.VMEM((rows, cols, chans), jnp.bfloat16),
            pltpu.VMEM((VIEWS, rows + 2, wide, chans), jnp.bfloat16),
            pltpu.VMEM((groups, 3, depth, 3 * width), jnp.bfloat16),
            pltpu.VMEM((groups, rows * wide, 2 * width), jnp.float32),
            pltpu.VMEM((groups, rows * cols, width), jnp.float32),
            dma,
            dma((groups * taps,)),
            dma((2, VIEWS, CHUNKS)),
            dma((VIEWS, CHUNKS)),
            dma((2, VIEWS, CHUNKS)),
            dma((2, VIEWS, CHUNKS)),
            dma((2, VIEWS)),
            dma((2, VIEWS)),
        ],
        compiler_params=pltpu.CompilerParams(
            collective_id=0, has_side_effects=True, vmem_limit_bytes=40 << 20),
    )(coords, offsets, src_feat[0], weights[0])
    return out[None]


def solution(mesh):
    sizes = (mesh.shape["shard"], mesh.shape["slab"])
    in_specs = (
        P("src", "slab", "shard", None),
        P("src", None),
        P("slab"),
        P("src", None, None, None, None),
    )
    out_specs = P("src", "slab", "shard", None)
    return jax.shard_map(functools.partial(local, sizes), mesh=mesh, in_specs=in_specs, out_specs=out_specs,
                         check_vma=False)
```

time: 107 us -> 48.9 us (0.46)
  waiting for transfers between devices: 53.6 us -> 0 us
  Pallas kernels: 0 us -> 44.1 us
  between operations: 15.6 us -> 0.67 us
  starting transfers between devices: 14.2 us -> 0 us
  local copies, waits for them, and re-layouts: 14.4 us -> 3.97 us
  other arithmetic: 4.85 us -> 0 us
  matrix products: 3.96 us -> 0 us
    pallas_call x0 -> x1, Pallas kernels: none -> 44.1 us  [local(): pl.pallas_call(functools.partial(kernel, sizes), out_shape=jax.ShapeDtype...]
    all_gather x1 -> x0, waiting for transfers between devices: 41 us -> none  [local(): all_views = lax.all_gather(posed, 'src', axis=0, tiled=True)]
    ppermute x4 -> x0, starting transfers between devices: 14.2 us -> none  [the longest x2 10.4 us: with_halo(): before = lax.ppermute(last, axis, up)]
    ppermute x4 -> x0, waiting for transfers between devices: 12.5 us -> none  [the longest x2 12.5 us: with_halo(): after = lax.ppermute(leading, axis, down)]
    slice x3 -> x0, local copies, waits for them, and re-layouts: 12.1 us -> none  [the longest x1 10.1 us: local(): grouped[:, tap_row:tap_row + row_count, tap_col:tap_col + col_count, :]]
    dot_general x9 -> x0, matrix products: 3.96 us -> none  [local(): jnp.einsum('grcn,tgno->tgrco', window, weights[:, :, tap_index], preferre...]
    unnamed x6 -> x7, local copies, waits for them, and re-layouts: 0.01 us -> 3.97 us
    convert_element_type x3 -> x0, other arithmetic: 2.72 us -> none  [the longest x1 1.71 us: local(): (src_feat.astype(jnp.float32) + encoded[None, :, None, :]).astype(jnp.bfl...]
  transfers between devices with their start and end apart: 5 -> 0, of which waited for: 3 -> 0; matrix products, arithmetic and copies ran while one was open for 1% -> 0% of each run, Pallas kernels for 0% -> 0%
where the time goes in v1:
time: 48.9 us; the launch traced here: 48.7 us
  Pallas kernels  44.1 us (90%)
  local copies, waits for them, and re-layouts  3.97 us (8%)
  between operations  0.67 us (1%)
    pallas_call x1, Pallas kernels, local(): pl.pallas_call(functools.partial(kernel, sizes), out_shape=jax.ShapeDtype...  44.1 us
    unnamed x7, local copies, waits for them, and re-layouts  3.97 us

profile of v1, /device:TPU:31, one launch (start us, length us, event | category | flops | bytes accessed | tf_op | source)
XLA Modules:
  0.0 48.7 jit_solution(17585754974993874836)
XLA Ops:
  0.7 0.0 copy-start
  0.7 1.7 %copy-done = bf16[1,2,9,512,128]{4,3,2,1,0:T(8,128)(2,1)S(1)} copy-done((bf16[1,2,9,512,128]{4,3,2,1,0:T(8,128)(2,1)S(1)}, bf16[1,2,9,512,128]{4,3,2,1,0:T(8,128)(2,1)}, u32[]{:S(2)}) %copy-start) | copy-done | bytes 2359320
  2.3 0.0 copy-start.1
  2.3 0.9 %copy-done.1 = bf16[1,32,16,256]{3,2,1,0:T(8,128)(2,1)S(1)} copy-done((bf16[1,32,16,256]{3,2,1,0:T(8,128)(2,1)S(1)}, bf16[1,32,16,256]{3,2,1,0:T(8,128)(2,1)}, u32[]{:S(2)}) %copy-start.1) | copy-done | bytes 262168
  3.3 0.0 copy-start.2
  3.3 0.7 %copy-done.2 = s32[1,2]{1,0:T(1,128)S(1)} copy-done((s32[1,2]{1,0:T(1,128)S(1)}, s32[1,2]{1,0:T(1,128)}, u32[]{:S(2)}) %copy-start.2) | copy-done | bytes 32
  3.9 44.1 %shard_map.46 = bf16[32,16,256]{2,1,0:T(8,128)(2,1)S(1)} custom-call(s32[1,2]{1,0:T(1,128)S(1)} %copy-done.2, s32[1]{0:T(128)S(6)} %copy.6.offsets_ref, bf16[32,16,256]{2,1,0:T(8,128)(2,1)S(1)} %bitcast.5, bf16[2,9,512,128]{3,2,1,0:T(8,128)(2,1)S(1)} %bitcast.3), custom_call_target="tpu_custom_call" | custom-call | tf_op jit(solution)/shard_map/pallas_call | solution.py:230
  48.0 0.7 %copy.7 = bf16[1,32,16,256]{3,2,1,0:T(8,128)(2,1)} copy(bf16[1,32,16,256]{3,2,1,0:T(8,128)(2,1)S(1)} %bitcast.4) | data formatting | bytes 524288
Async XLA Ops:
  0.7 1.7 %copy-start = (bf16[1,2,9,512,128]{4,3,2,1,0:T(8,128)(2,1)S(1)}, bf16[1,2,9,512,128]{4,3,2,1,0:T(8,128)(2,1)}, u32[]{:S(2)}) copy-start(bf16[1,2,9,512,128]{4,3,2,1,0:T(8,128)(2,1)} %param.7) | copy-start | bytes 7077892
  2.3 0.9 %copy-start.1 = (bf16[1,32,16,256]{3,2,1,0:T(8,128)(2,1)S(1)}, bf16[1,32,16,256]{3,2,1,0:T(8,128)(2,1)}, u32[]{:S(2)}) copy-start(bf16[1,32,16,256]{3,2,1,0:T(8,128)(2,1)} %param.4) | copy-start | bytes 786436
  3.3 0.7 %copy-start.2 = (s32[1,2]{1,0:T(1,128)S(1)}, s32[1,2]{1,0:T(1,128)}, u32[]{:S(2)}) copy-start(s32[1,2]{1,0:T(1,128)} %coords_ref.1) | copy-start | bytes 28

commit v2 on v1

v2 whole, which is shorter than its diff:
```python
import functools
import math

import jax
import jax.numpy as jnp
from jax import lax
from jax.experimental import pallas as pl
from jax.experimental.pallas import tpu as pltpu
from jax.sharding import PartitionSpec as P

VIEWS = 4
CHUNKS = 4
EDGE = 8
MESH = pl.DeviceIdType.MESH


def encoding(offset, first_row, row_count, chans):
    row_idx = lax.broadcasted_iota(jnp.int32, (row_count, chans), 0)
    rowpos = (offset + first_row + row_idx).astype(jnp.float32)
    chan = lax.broadcasted_iota(jnp.int32, (row_count, chans), 1)
    halves = (chan // 2).astype(jnp.float32)
    frequency = jnp.exp(-math.log(1000.0) * halves / (chans / 2))
    phases = (chan % 2).astype(jnp.float32) * (math.pi / 2)
    return jnp.sin(rowpos * frequency + phases)


def count(*conditions):
    return sum(condition.astype(jnp.int32) for condition in conditions)


def kernel(sizes, coords_ref, offsets_ref, src_hbm, w_hbm, out_hbm, src, panel, halo, weights, side_acc, mid_acc,
           blend, out, src_sem, w_sem, out_sem, z_send, z_recv, col_send, col_recv, row_send, row_recv, cross_send,
           z_ready, col_ready, row_ready, cross_ready):
    shards, slabs = sizes
    rows, cols, chans = src.shape
    groups, _, depth, width = w_hbm.shape[0], None, w_hbm.shape[2], w_hbm.shape[3]
    wide = cols + 2 * EDGE
    step_rows = rows // CHUNKS
    s, h, b = lax.axis_index("src"), lax.axis_index("shard"), lax.axis_index("slab")
    below, above = s > 0, s < VIEWS - 1
    has_left, has_right = h > 0, h < shards - 1
    has_top, has_bottom = b > 0, b < slabs - 1
    cross_bottom, cross_top = b == slabs // 2 - 1, b == slabs // 2
    near_top, near_bottom = has_top & jnp.logical_not(cross_top), has_bottom & jnp.logical_not(cross_bottom)

    def signal(sem, target):
        pl.semaphore_signal(sem, inc=1, device_id=target, device_id_type=MESH)

    src_copy = pltpu.make_async_copy(src_hbm, src, src_sem)
    src_copy.start()

    barrier = pltpu.get_barrier_semaphore()
    for present, targets in (
        (below, ({"src": s - 1},)),
        (has_left, ({"shard": h - 1},)),
        (near_top, ({"slab": b - 1},)),
        (cross_bottom, tuple({"src": t, "slab": b + 1} for t in range(VIEWS))),
    ):
        @pl.when(present)
        def _():
            for target in targets:
                signal(barrier, target)
    expected = count(above, has_right, near_bottom) + VIEWS * count(cross_top)

    @pl.when(expected > 0)
    def _():
        pl.semaphore_wait(barrier, expected)

    for present, sem, targets in (
        (above, z_ready, ({"src": s + 1},)),
        (has_right, col_ready, ({"shard": h + 1},)),
        (near_bottom, row_ready, ({"slab": b + 1},)),
        (cross_top, cross_ready, tuple({"src": t, "slab": b - 1} for t in range(VIEWS))),
    ):
        @pl.when(present)
        def _():
            for target in targets:
                signal(sem, target)

    def weight_copy(i):
        g, tap = i // 9, i % 9
        lane = (0, 2, 1)[tap % 3] * width
        return pltpu.make_async_copy(
            w_hbm.at[g, tap], weights.at[g, tap // 3, :, lane:lane + width], w_sem.at[i])

    def chunk_start(k):
        return ((CHUNKS - 1) * k) % CHUNKS * step_rows

    def z_copy(v, k, up):
        part = panel.at[v, pl.ds(chunk_start(k), step_rows), 0:cols, :]
        return pltpu.make_async_remote_copy(
            src_ref=part, dst_ref=part, send_sem=z_send.at[up, v, k], recv_sem=z_recv.at[v, k],
            device_id={"src": s + 1 if up else s - 1}, device_id_type=MESH)

    def col_copy(v, k, right):
        at = pl.ds(chunk_start(k), step_rows)
        part = panel.at[v, at, cols - EDGE:cols, :] if right else panel.at[v, at, 0:EDGE, :]
        into = panel.at[v, at, cols:cols + EDGE, :] if right else panel.at[v, at, cols + EDGE:, :]
        return pltpu.make_async_remote_copy(
            src_ref=part, dst_ref=into, send_sem=col_send.at[right, v, k], recv_sem=col_recv.at[right, v, k],
            device_id={"shard": h + 1 if right else h - 1}, device_id_type=MESH)

    def row_copy(v, down):
        return pltpu.make_async_remote_copy(
            src_ref=panel.at[v, rows - 1 if down else 0], dst_ref=halo.at[1 - down, v],
            send_sem=row_send.at[down, v], recv_sem=row_recv.at[down, v],
            device_id={"slab": b + 1 if down else b - 1}, device_id_type=MESH)

    def cross_copy(t, down):
        return pltpu.make_async_remote_copy(
            src_ref=panel.at[s, rows - 1 if down else 0], dst_ref=halo.at[1 - down, s],
            send_sem=cross_send.at[t], recv_sem=row_recv.at[down, s],
            device_id={"src": t, "slab": b + 1 if down else b - 1}, device_id_type=MESH)

    vertical = coords_ref[0, 0].astype(jnp.float32) / 6.0
    across = coords_ref[0, 1].astype(jnp.float32) / 6.0

    def multiply(v, k):
        for right, present in ((1, has_left), (0, has_right)):
            @pl.when(present)
            def _():
                col_copy(v, k, right).wait_recv()

        g = v // 2
        start = chunk_start(k)
        at = pl.ds(start, step_rows)
        taken = pl.ds(pl.multiple_of((v % 2) * chans, chans), chans)
        full = panel[v, at, :, :].reshape(step_rows * wide, chans)
        own = panel[v, at, 0:cols, :]
        flat = own.reshape(step_rows * cols, chans)
        for a in range(3):
            side_at = pl.ds(pl.multiple_of((start + 2 - a) * wide, wide), step_rows * wide)
            side_acc[g, side_at, :] += jnp.dot(
                full, weights[g, a, taken, 0:2 * width], preferred_element_type=jnp.float32)
            mid_at = pl.ds(pl.multiple_of((start + 2 - a) * cols, cols), step_rows * cols)
            mid_acc[g, mid_at, :] += jnp.dot(
                flat, weights[g, a, taken, 2 * width:], preferred_element_type=jnp.float32)
        mix = jnp.where(v >= 2, vertical, 1.0 - vertical) * jnp.where(v % 2 == 1, across, 1.0 - across)
        blend[at] += mix * own.astype(jnp.float32)

    def send_rows(v):
        @pl.when(near_top)
        def _():
            row_copy(v, 0).start()

        @pl.when(near_bottom)
        def _():
            row_copy(v, 1).start()

    def multiply_rows(v):
        g = v // 2
        taken = pl.ds(pl.multiple_of((v % 2) * chans, chans), chans)
        for from_top, present, a, row in ((1, has_top, 0, 1), (0, has_bottom, 2, rows)):
            @pl.when(present)
            def _():
                row_copy(v, from_top).wait_recv()
                line = halo[1 - from_top, v]
                side_acc[g, row * wide:(row + 1) * wide, :] += jnp.dot(
                    line, weights[g, a, taken, 0:2 * width], preferred_element_type=jnp.float32)
                mid_acc[g, row * cols:(row + 1) * cols, :] += jnp.dot(
                    line[0:cols], weights[g, a, taken, 2 * width:], preferred_element_type=jnp.float32)

    def for_views(step, act):
        @pl.when(s - step >= 0)
        def _():
            act(s - step, 1)

        @pl.when((step > 0) & (s + step < VIEWS))
        def _():
            act(s + step, 0)

    src_copy.wait()

    @pl.loop(0, CHUNKS)
    def _(k):
        start = chunk_start(k)
        at = pl.ds(start, step_rows)
        encoded = encoding(offsets_ref[0], start, step_rows, chans)
        panel[s, at, 0:cols, :] = (src[at].astype(jnp.float32) + encoded[:, None, :]).astype(panel.dtype)

        @pl.when(above)
        def _():
            z_copy(s, k, 1).start()

        @pl.when(has_right)
        def _():
            col_copy(s, k, 1).start()

    @pl.when(below)
    def _():
        pl.semaphore_wait(z_ready, 1)

        @pl.loop(0, CHUNKS)
        def _(k):
            z_copy(s, k, 0).start()

    for i in range(groups * 9):
        weight_copy(i).start()

    @pl.when(has_left)
    def _():
        pl.semaphore_wait(col_ready, 1)

        @pl.loop(0, CHUNKS)
        def _(k):
            col_copy(s, k, 0).start()

    side_acc[...] = jnp.zeros_like(side_acc)
    mid_acc[...] = jnp.zeros_like(mid_acc)
    blend[...] = jnp.zeros_like(blend)

    @pl.when(jnp.logical_not(has_left))
    def _():
        panel[:, :, cols:cols + EDGE, :] = jnp.zeros((VIEWS, rows, EDGE, chans), panel.dtype)

    @pl.when(jnp.logical_not(has_right))
    def _():
        panel[:, :, cols + EDGE:, :] = jnp.zeros((VIEWS, rows, EDGE, chans), panel.dtype)

    for i in range(groups * 9):
        weight_copy(i).wait()

    @pl.loop(0, CHUNKS)
    def _(k):
        multiply(s, k)

        @pl.when((k == 0) & cross_top)
        def _():
            for t in range(VIEWS):
                cross_copy(t, 0).start()

    items = VIEWS * CHUNKS

    @pl.loop(CHUNKS, items + 1)
    def _(i):
        k = i % CHUNKS

        def arrive(v, up):
            z_copy(v, k, up).wait_recv()

            @pl.when(above if up else below)
            def _():
                z_copy(v, k, up).start()

            for right, present in ((1, has_right), (0, has_left)):
                @pl.when(present)
                def _():
                    col_copy(v, k, right).start()

        @pl.when(i < items)
        def _():
            for_views(i // CHUNKS, arrive)

        @pl.when(i == items)
        def _():
            for_views(VIEWS - 1, lambda v, up: multiply_rows(v))

        @pl.when(i > CHUNKS)
        def _():
            for_views((i - 1) // CHUNKS, lambda v, up: multiply(v, (i - 1) % CHUNKS))

        @pl.when(i == 2 * CHUNKS + 1)
        def _():
            @pl.when(near_top)
            def _():
                pl.semaphore_wait(row_ready, 1)

            @pl.when(cross_bottom)
            def _():
                pl.semaphore_wait(cross_ready, VIEWS)
                for t in range(VIEWS):
                    cross_copy(t, 1).start()

            for_views(0, lambda v, up: send_rows(v))
            for_views(1, lambda v, up: send_rows(v))

        @pl.when((i == 2 * CHUNKS + 2) | (i == 3 * CHUNKS + 2))
        def _():
            for_views(i // CHUNKS, lambda v, up: send_rows(v))

        @pl.when(i == 3 * CHUNKS + 2)
        def _():
            @pl.loop(0, VIEWS - 1)
            def _(step):
                for_views(step, lambda v, up: multiply_rows(v))

    def out_copy(j):
        at = pl.ds(j * EDGE, EDGE)
        return pltpu.make_async_copy(out.at[at], out_hbm.at[at], out_sem.at[j])

    @pl.loop(0, rows // EDGE)
    def _(j):
        at = pl.ds(j * EDGE, EDGE)
        for g in range(groups):
            lanes = slice(g * width, (g + 1) * width)
            side = side_acc[g, pl.ds(pl.multiple_of((j * EDGE + 1) * wide, wide), EDGE * wide), :]
            side = side.reshape(EDGE, wide, 2 * width)
            joined = mid_acc[g, pl.ds(pl.multiple_of((j * EDGE + 1) * cols, cols), EDGE * cols), :]
            joined = joined.reshape(EDGE, cols, width)
            joined += jnp.concatenate(
                [side[:, cols + EDGE - 1:cols + EDGE, :width], side[:, 0:cols - 1, :width]], axis=1)
            joined += jnp.concatenate(
                [side[:, 1:cols, width:], side[:, cols + EDGE:cols + EDGE + 1, width:]], axis=1)
            blended = blend[at, :, lanes]
            out[at, :, lanes] = (blended + joined / (1.0 + jnp.exp(-joined))).astype(out.dtype)
        out_copy(j).start()

    @pl.loop(0, CHUNKS)
    def _(k):
        out_copy(k).wait()
        for v in range(VIEWS):
            @pl.when(above & (s >= v))
            def _():
                z_copy(v, k, 1).wait_send()

            @pl.when(below & (s <= v))
            def _():
                z_copy(v, k, 0).wait_send()

            for right, present in ((1, has_right), (0, has_left)):
                @pl.when(present)
                def _():
                    col_copy(v, k, right).wait_send()

    @pl.loop(0, VIEWS)
    def _(v):
        for down, present in ((1, near_bottom), (0, near_top)):
            @pl.when(present)
            def _():
                row_copy(v, down).wait_send()

        for down, present in ((1, cross_bottom), (0, cross_top)):
            @pl.when(present)
            def _():
                cross_copy(v, down).wait_send()


def local(sizes, src_feat, coords, offsets, weights):
    _, rows, cols, chans = src_feat.shape
    _, groups, taps, depth, width = weights.shape
    wide = cols + 2 * EDGE
    dma, regular = pltpu.SemaphoreType.DMA, pltpu.SemaphoreType.REGULAR
    out = pl.pallas_call(
        functools.partial(kernel, sizes),
        out_shape=jax.ShapeDtypeStruct((rows, cols, chans), jnp.bfloat16),
        in_specs=[
            pl.BlockSpec(memory_space=pltpu.SMEM),
            pl.BlockSpec(memory_space=pltpu.SMEM),
            pl.BlockSpec(memory_space=pltpu.HBM),
            pl.BlockSpec(memory_space=pltpu.HBM),
        ],
        out_specs=pl.BlockSpec(memory_space=pltpu.HBM),
        scratch_shapes=[
            pltpu.VMEM((rows, cols, chans), jnp.bfloat16),
            pltpu.VMEM((VIEWS, rows, wide, chans), jnp.bfloat16),
            pltpu.VMEM((2, VIEWS, wide, chans), jnp.bfloat16),
            pltpu.VMEM((groups, 3, depth, 3 * width), jnp.bfloat16),
            pltpu.VMEM((groups, (rows + 2) * wide, 2 * width), jnp.float32),
            pltpu.VMEM((groups, (rows + 2) * cols, width), jnp.float32),
            pltpu.VMEM((rows, cols, chans), jnp.float32),
            pltpu.VMEM((rows, cols, chans), jnp.bfloat16),
            dma,
            dma((groups * taps,)),
            dma((CHUNKS,)),
            dma((2, VIEWS, CHUNKS)),
            dma((VIEWS, CHUNKS)),
            dma((2, VIEWS, CHUNKS)),
            dma((2, VIEWS, CHUNKS)),
            dma((2, VIEWS)),
            dma((2, VIEWS)),
            dma((VIEWS,)),
            regular,
            regular,
            regular,
            regular,
        ],
        compiler_params=pltpu.CompilerParams(
            collective_id=0, has_side_effects=True, vmem_limit_bytes=60 << 20),
    )(coords, offsets, src_feat[0], weights[0])
    return out[None]


def solution(mesh):
    sizes = (mesh.shape["shard"], mesh.shape["slab"])
    in_specs = (
        P("src", "slab", "shard", None),
        P("src", None),
        P("slab"),
        P("src", None, None, None, None),
    )
    out_specs = P("src", "slab", "shard", None)
    return jax.shard_map(functools.partial(local, sizes), mesh=mesh, in_specs=in_specs, out_specs=out_specs,
                         check_vma=False)
```

time: 48.9 us -> 38.6 us (0.79)
  Pallas kernels: 44.1 us -> 36 us
  local copies, waits for them, and re-layouts: 3.97 us -> 1.67 us
    pallas_call x1, Pallas kernels: 44.1 us -> 36 us  [local(): pl.pallas_call(functools.partial(kernel, sizes), out_shape=jax.ShapeDtype...]
    unnamed x7 -> x1, local copies, waits for them, and re-layouts: 3.97 us -> 1.67 us
where the time goes in v2:
time: 38.6 us; the launch traced here: 38.4 us
  Pallas kernels  36 us (93%)
  local copies, waits for them, and re-layouts  1.67 us (4%)
  between operations  0.66 us (2%)
    pallas_call x1, Pallas kernels, local(): pl.pallas_call(functools.partial(kernel, sizes), out_shape=jax.ShapeDtype...  36 us
    unnamed x1, local copies, waits for them, and re-layouts  1.67 us

profile of v2, /device:TPU:31, one launch (start us, length us, event | category | flops | bytes accessed | tf_op | source)
XLA Modules:
  0.0 38.4 jit_solution(16086655341726777301)
XLA Ops:
  0.7 36.0 %shard_map.46 = bf16[32,16,256]{2,1,0:T(8,128)(2,1)} custom-call(s32[1,2]{1,0:T(1,128)} %coords_ref.1, s32[1]{0:T(128)S(6)} %copy.6.offsets_ref, bf16[32,16,256]{2,1,0:T(8,128)(2,1)} %bitcast.5, bf16[2,9,512,128]{3,2,1,0:T(8,128)(2,1)} %bitcast.3), custom_call_target="tpu_custom_call" | custom-call | tf_op jit(solution)/shard_map/pallas_call | solution.py:343
  36.7 1.7 %copy.7 = bf16[1,32,16,256]{3,2,1,0:T(8,128)(2,1)} copy(bf16[1,32,16,256]{3,2,1,0:T(8,128)(2,1)} %bitcast.4) | data formatting | bytes 524288
